TPU v7x, 256 devices: a whole 4x4x8 slice. The times are simulated.
256 devices in a mesh: blk: 64 (over z, y, x_hi), pb: 4 (over x_lo, core).
Axes of the slice: x: 4 (x_hi: 2, x_lo: 2; x = x_hi * 2 + x_lo), y: 4, z: 8, core: 2. Of those that a mesh axis runs over, the one named last changes fastest.
Arguments:
- query_rows: bfloat16 [81920, 1024], P(('blk', 'pb')), may hold values from -64 to 64
- key_rows: bfloat16 [81920, 1024], P(('blk', 'pb')), may hold values from -64 to 64
- partner: int32 [64, 1280], P('blk', 'pb'), may hold values from 0 to 1279, each once within a row
Outputs:
- pair_loss: float32 [81920], P(('blk', 'pb'))
- grad_queries: float32 [81920, 1024], P(('blk', 'pb'))
- grad_keys: float32 [81920, 1024], P(('blk', 'pb'))
Inputs may be any that keep to these rules, and one draw needn't show every extreme that they name: Each row of partner is a permutation of 0 .. 1279.
All inputs are finite; a program needn't handle non-finite values.
Results may differ from a plain program's by a relative error of at most 0.0015.
Values may be sent and summed in bfloat16 or wider, within the bound.
A program may use at most 192 MiB of HBM per device.

v0:
```python
import jax
import jax.numpy as jnp
from jax import lax
from jax.sharding import PartitionSpec as P

WIN = 4


def from_behind(array, axis, by):
    peers = lax.axis_size(axis)
    return lax.ppermute(array, axis, [(i, (i + by) % peers) for i in range(peers)])


def joined(array, axis, combine):
    everything = jax.tree.map(lambda part: lax.all_gather(part, axis), array)
    leading = jax.tree.map(lambda part: part[0], everything)

    def hop(k, so_far):
        return combine(so_far, jax.tree.map(lambda part: part[k], everything))

    return lax.fori_loop(1, lax.axis_size(axis), hop, leading)


def merge_pairs(first, second):
    first_max, first_sum = first
    second_max, second_sum = second
    top = jnp.maximum(first_max, second_max)
    return (top, first_sum * jnp.exp(first_max - top) + second_sum * jnp.exp(second_max - top))


def add_logs(first, second):
    top = jnp.maximum(first, second)
    return top + jnp.log(jnp.exp(first - top) + jnp.exp(second - top))


def local(query_rows, key_rows, partner):
    features = query_rows.shape[1]
    factor = float(features) ** (-0.5)
    block_keys = lax.all_gather(key_rows, "pb", axis=0, tiled=True)
    pieces = [block_keys]
    arrived = block_keys
    for step in range(1, WIN):
        arrived = from_behind(arrived, "blk", 1)
        pieces.append(arrived)
    window_keys = jnp.stack(pieces)
    block_size = window_keys.shape[1]
    scores = (
        jnp.einsum("qd,skd->sqk", query_rows, window_keys, preferred_element_type=jnp.float32)
        * factor
    )
    row_max = jnp.max(scores, axis=(0, 2))
    row_lse = row_max + jnp.log(jnp.sum(jnp.exp(scores - row_max[None, :, None]), axis=(0, 2)))
    col_max = jnp.max(scores, axis=1)
    col_sum = jnp.sum(jnp.exp(scores - col_max[:, None, :]), axis=1)
    col_max, col_sum = joined((col_max, col_sum), "pb", merge_pairs)
    partial_lse = col_max + jnp.log(col_sum)
    carried = partial_lse[WIN - 1]
    for step in range(WIN - 2, -1, -1):
        arrived_lse = from_behind(carried, "blk", -1)
        carried = add_logs(arrived_lse, partial_lse[step])
    lse_list = [carried]
    travelling = carried
    for step in range(1, WIN):
        travelling = from_behind(travelling, "blk", 1)
        lse_list.append(travelling)
    col_lse = jnp.stack(lse_list)
    chosen = partner[0]
    columns = jnp.arange(block_size, dtype=jnp.int32)
    mask = (columns[None, :] == chosen[:, None]).astype(jnp.float32)
    first_only = (jnp.arange(WIN, dtype=jnp.int32) == 0).astype(jnp.float32)
    weights = 0.5 * jnp.exp(scores - row_lse[None, :, None]) + 0.5 * jnp.exp(
        scores - col_lse[:, None, :]
    )
    weights = (weights - first_only[:, None, None] * mask[None, :, :]).astype(jnp.bfloat16)
    positive = jnp.take_along_axis(scores[0], chosen[:, None], axis=1)[:, 0]
    pair_loss = 0.5 * row_lse + 0.5 * jnp.take(col_lse[0], chosen) - positive
    grad_queries = (
        jnp.einsum("sqk,skd->qd", weights, window_keys, preferred_element_type=jnp.float32) * factor
    )
    partials = jnp.einsum("sqk,qd->skd", weights, query_rows, preferred_element_type=jnp.float32)
    summed = partials[0]
    for step in range(1, WIN):
        summed = summed + from_behind(partials[step], "blk", -step)
    grad_keys = lax.psum_scatter(summed, "pb", scatter_dimension=0, tiled=True)
    return (pair_loss, grad_queries, grad_keys * factor)


def solution(mesh):
    return jax.shard_map(
        local,
        mesh=mesh,
        in_specs=(P(("blk", "pb"), None), P(("blk", "pb"), None), P("blk", "pb")),
        out_specs=(P(("blk", "pb")), P(("blk", "pb"), None), P(("blk", "pb"), None)),
        check_vma=False,
    )
```

profile of v0, /device:TPU:1, one launch (start us, length us, event | category | flops | bytes accessed | tf_op | source)
XLA Modules:
  0.0 921.1 jit_solution(18166864339300178444)
XLA Ops:
  7.2 0.0 copy-start
  7.2 0.0 all-gather.6.cloned.1.call-start
  7.2 0.7 all-gather.6.cloned.1.call-update
  7.9 0.0 reduce-scatter.2.cloned.1.call-start
  8.0 42.1 %all-gather.6.cloned.1.call-done = bf16[1280,1024]{1,0:T(8,128)(2,1)} async-done(((bf16[320,1024]{1,0:T(8,128)(2,1)}), bf16[1280,1024]{1,0:T(8,128)(2,1)}) %all-gather.6.cloned.1.call-update) | async-done | bytes 2621456 | tf_op jit(solution)/shard_map/all_gather | solution.py:39
  50.0 2.4 collective-permute-start
  52.4 62.4 %collective-permute-done = bf16[1280,1024]{1,0:T(8,128)(2,1)S(1)} collective-permute-done((bf16[1280,1024]{1,0:T(8,128)(2,1)}, bf16[1280,1024]{1,0:T(8,128)(2,1)S(1)}, u32[]{:S(2)}, u32[]{:S(2)}) %collective-permute-start) | collective-permute-done | bytes 2621472 | tf_op jit(solution)/shard_map/ppermute | solution.py:11
  114.8 1.5 copy-done.5
  116.3 63.7 %collective-permute-done.1 = bf16[1280,1024]{1,0:T(8,128)(2,1)} collective-permute-done((bf16[1280,1024]{1,0:T(8,128)(2,1)S(1)}, bf16[1280,1024]{1,0:T(8,128)(2,1)}, u32[]{:S(2)}, u32[]{:S(2)}) %collective-permute-start.1) | collective-permute-done | bytes 2621472 | tf_op jit(solution)/shard_map/ppermute | solution.py:11
  180.1 0.7 reduce.1
  180.8 0.7 compare_select_fusion
  181.5 1.3 fusion.7
  182.8 60.3 %collective-permute-done.2 = bf16[1280,1024]{1,0:T(8,128)(2,1)} collective-permute-done((bf16[1280,1024]{1,0:T(8,128)(2,1)}, bf16[1280,1024]{1,0:T(8,128)(2,1)}, u32[]{:S(2)}, u32[]{:S(2)}) %collective-permute-start.2) | collective-permute-done | bytes 2621472 | tf_op jit(solution)/shard_map/ppermute | solution.py:11
  243.1 7.3 fusion.23
  250.5 7.4 all-gather.2
  257.8 3.5 multiply_reduce_fusion
  261.3 2.6 exponential_reduce_fusion
  263.9 5.4 all-gather.3
  269.3 0.2 while.17
  269.5 0.1 slice_reduce_fusion.3
  269.5 0.1 collective-permute-start.3
  269.7 4.0 collective-permute-done.3
  273.6 4.3 collective-permute-start.4
  278.0 0.8 collective-permute-done.4
  278.7 7.5 collective-permute-start.5
  286.3 0.8 collective-permute-done.5
  287.1 0.1 collective-permute-start.6
  287.2 8.4 collective-permute-done.6
  295.6 1.5 slice_bitcast_fusion.4
  297.2 3.0 gather_fusion.1
  300.2 2.2 gather_fusion
  302.4 1.4 collective-permute-done.7
  303.8 0.0 collective-permute-start.8
  303.8 0.6 select_subtract_fusion
  304.5 7.6 collective-permute-done.8
  312.1 16.3 %fusion.10 = f32[4,1280,1024]{2,1,0:T(8,128)} fusion(bf16[320,1024]{1,0:T(8,128)(2,1)S(1)} %copy-done, f32[320,1280]{1,0:T(8,128)} %fusion.7, f32[4]{0:T(128)S(1)} %compare_convert_fusion, f32[4,1280]{1,0:T(4,128)S(1)} %pad_maximum_fusion.7, f32[320]{0:T(512)S(1)} %get-tuple-element.157, f32[4,1280,320]{1,2,0:T(8,128)} %copy-done.2), kind=kOutput, calls=%fused_computation.27 | convolution fusion | flops 3368550400 | bytes 29840656 | tf_op jit(solution)/shard_map/sqk,qd->skd/dot_general | solution.py:80
  328.4 12.4 %slice_bitcast_fusion.2 = (f32[1280,1024]{1,0:T(8,128)}, f32[1280,1024]{1,0:T(8,128)}, f32[1280,1024]{1,0:T(8,128)}) fusion(f32[4,1280,1024]{2,1,0:T(8,128)} %fusion.10), kind=kLoop, calls=%fused_computation.15 | loop fusion | bytes 31457280 | tf_op jit(solution)/shard_map/squeeze | solution.py:83
  340.8 1.8 collective-permute-start.9
  342.6 0.0 collective-permute-start.10
  342.6 266.5 %collective-permute-done.9 = f32[1280,1024]{1,0:T(8,128)} collective-permute-done((f32[1280,1024]{1,0:T(8,128)}, f32[1280,1024]{1,0:T(8,128)}, u32[]{:S(2)}, u32[]{:S(2)}) %collective-permute-start.9) | collective-permute-done | bytes 5242912 | tf_op jit(solution)/shard_map/ppermute | solution.py:11
  609.1 116.6 %collective-permute-done.11 = f32[1280,1024]{1,0:T(8,128)} collective-permute-done((f32[1280,1024]{1,0:T(8,128)}, f32[1280,1024]{1,0:T(8,128)}, u32[]{:S(2)}, u32[]{:S(2)}) %collective-permute-start.11) | collective-permute-done | bytes 5242912 | tf_op jit(solution)/shard_map/ppermute | solution.py:11
  725.7 112.4 %collective-permute-done.10 = f32[1280,1024]{1,0:T(8,128)} collective-permute-done((f32[1280,1024]{1,0:T(8,128)}, f32[1280,1024]{1,0:T(8,128)}, u32[]{:S(2)}, u32[]{:S(2)}) %collective-permute-start.10) | collective-permute-done | bytes 5242912 | tf_op jit(solution)/shard_map/ppermute | solution.py:11
  838.1 12.6 %fusion.4 = f32[1280,1024]{1,0:T(8,128)} fusion(f32[1280,1024]{1,0:T(8,128)} %collective-permute-done.11, f32[1280,1024]{1,0:T(8,128)} %collective-permute-done.10, f32[1280,1024]{1,0:T(8,128)} %collective-permute-done.9, f32[4,1280,1024]{2,1,0:T(8,128)} %fusion.10), kind=kLoop, calls=%fused_computation.19 | loop fusion | flops 3932160 | bytes 26214400 | tf_op jit(solution)/shard_map/add | solution.py:83
  850.6 0.0 reduce-scatter.2.cloned.1.call-update
  850.7 0.0 copy-start.1
  850.7 12.0 %fusion.9 = f32[320,1024]{1,0:T(8,128)} fusion(bf16[1,1280,1024]{2,1,0:T(8,128)(2,1)} %bitcast.5, bf16[1,1280,1024]{2,1,0:T(8,128)(2,1)} %bitcast.4, bf16[1,1280,1024]{2,1,0:T(8,128)(2,1)} %bitcast.74, bf16[1,1280,1024]{2,1,0:T(8,128)(2,1)} %bitcast.72, f32[320,1280]{1,0:T(8,128)S(1)} %copy-done.3, f32[4]{0:T(128)S(1)} %compare_convert_fusion, ...), kind=kOutput, calls=%fused_computation.26 | convolution fusion | flops 3384606720 | bytes 20010256 | tf_op jit(solution)/shard_map/sqk,skd->qd/dot_general | solution.py:78
  862.6 49.1 %reduce-scatter.2.cloned.1.call-done = f32[320,1024]{1,0:T(8,128)} async-done(((f32[1280,1024]{1,0:T(8,128)}), f32[320,1024]{1,0:T(8,128)}) %reduce-scatter.2.cloned.1.call-update) | async-done | bytes 1310736 | tf_op jit(solution)/shard_map/reduce_scatter | solution.py:84
  911.7 2.5 broadcast_multiply_fusion
  (33 shorter events, 0.3 us)
Async XLA Ops:
  7.2 236.0 %copy-start = (bf16[320,1024]{1,0:T(8,128)(2,1)S(1)}, bf16[320,1024]{1,0:T(8,128)(2,1)}, u32[]{:S(2)}) copy-start(bf16[320,1024]{1,0:T(8,128)(2,1)} %param.5) | copy-start | bytes 1966084
  7.2 42.8 %all-gather.6.cloned.1.call-start = ((), (), s32[]{:S(2)}) async-start(), calls=%async_computation.1 | async-start | bytes 3276800 | tf_op jit(solution)/shard_map/all_gather | solution.py:39
  7.9 903.8 %reduce-scatter.2.cloned.1.call-start = ((), (), s32[]{:S(2)}) async-start(), calls=%async_computation.2 | async-start | bytes 6553600 | tf_op jit(solution)/shard_map/reduce_scatter | solution.py:84
  50.0 64.8 %collective-permute-start = (bf16[1280,1024]{1,0:T(8,128)(2,1)}, bf16[1280,1024]{1,0:T(8,128)(2,1)S(1)}, u32[]{:S(2)}, u32[]{:S(2)}) collective-permute-start(bf16[1280,1024]{1,0:T(8,128)(2,1)} %all-gather.6.cloned.1.call-done), channel_id=1, source_target_pairs={{0,4},{4,8},{8,12},{12,16},{16,20},{20,24},{24,28},{28,32},{32,36}... | collective-permute-start | bytes 7864328 | tf_op jit(solution)/shard_map/ppermute | solution.py:11
  114.8 1.5 copy-start.5
  116.3 63.7 %collective-permute-start.1 = (bf16[1280,1024]{1,0:T(8,128)(2,1)S(1)}, bf16[1280,1024]{1,0:T(8,128)(2,1)}, u32[]{:S(2)}, u32[]{:S(2)}) collective-permute-start(bf16[1280,1024]{1,0:T(8,128)(2,1)S(1)} %collective-permute-done), channel_id=1, source_target_pairs={{0,4},{4,8},{8,12},{12,16},{16,20},{20,24},{24,28},{28,32},{32,36}... | collective-permute-start | bytes 7864328 | tf_op jit(solution)/shard_map/ppermute | solution.py:11
  180.1 63.1 %collective-permute-start.2 = (bf16[1280,1024]{1,0:T(8,128)(2,1)}, bf16[1280,1024]{1,0:T(8,128)(2,1)}, u32[]{:S(2)}, u32[]{:S(2)}) collective-permute-start(bf16[1280,1024]{1,0:T(8,128)(2,1)} %collective-permute-done.1), channel_id=1, source_target_pairs={{0,4},{4,8},{8,12},{12,16},{16,20},{20,24},{24,28},{28,32},{32,36}... | collective-permute-start | bytes 7864328 | tf_op jit(solution)/shard_map/ppermute | solution.py:11
  250.4 10.9 %copy-start.2 = (f32[4,1280,320]{1,2,0:T(8,128)}, f32[4,1280,320]{1,2,0:T(8,128)S(1)}, u32[]{:S(2)}) copy-start(f32[4,1280,320]{1,2,0:T(8,128)S(1)} %get-tuple-element.164) | copy-start | bytes 19660804
  261.3 16.6 %copy-start.4 = (s32[1,320]{1,0:T(1,128)S(1)}, s32[1,320]{1,0:T(1,128)}, u32[]{:S(2)}) copy-start(s32[1,320]{1,0:T(1,128)} %param.7) | copy-start | bytes 3844
  269.5 4.1 collective-permute-start.3
  273.6 5.1 collective-permute-start.4
  278.7 8.3 collective-permute-start.5
  287.1 8.5 collective-permute-start.6
  295.6 8.2 collective-permute-start.7
  303.8 8.2 collective-permute-start.8
  340.8 268.3 %collective-permute-start.9 = (f32[1280,1024]{1,0:T(8,128)}, f32[1280,1024]{1,0:T(8,128)}, u32[]{:S(2)}, u32[]{:S(2)}) collective-permute-start(f32[1280,1024]{1,0:T(8,128)} %get-tuple-element.158), channel_id=1, source_target_pairs={{0,252},{4,0},{8,4},{12,8},{16,12},{20,16},{24,20},{28,24},{32,28}... | collective-permute-start | bytes 15728648 | tf_op jit(solution)/shard_map/ppermute | solution.py:11
  342.6 383.1 %collective-permute-start.11 = (f32[1280,1024]{1,0:T(8,128)}, f32[1280,1024]{1,0:T(8,128)}, u32[]{:S(2)}, u32[]{:S(2)}) collective-permute-start(f32[1280,1024]{1,0:T(8,128)} %get-tuple-element.159), channel_id=1, source_target_pairs={{0,244},{4,248},{8,252},{12,0},{16,4},{20,8},{24,12},{28,16},{32,2... | collective-permute-start | bytes 15728648 | tf_op jit(solution)/shard_map/ppermute | solution.py:11
  342.6 508.1 %copy-start.3 = (f32[320,1280]{1,0:T(8,128)S(1)}, f32[320,1280]{1,0:T(8,128)}, u32[]{:S(2)}) copy-start(f32[320,1280]{1,0:T(8,128)} %fusion.7) | copy-start | bytes 4915204
  342.6 495.5 %collective-permute-start.10 = (f32[1280,1024]{1,0:T(8,128)}, f32[1280,1024]{1,0:T(8,128)}, u32[]{:S(2)}, u32[]{:S(2)}) collective-permute-start(f32[1280,1024]{1,0:T(8,128)} %get-tuple-element.160), channel_id=1, source_target_pairs={{0,248},{4,252},{8,0},{12,4},{16,8},{20,12},{24,16},{28,20},{32,24... | collective-permute-start | bytes 15728648 | tf_op jit(solution)/shard_map/ppermute | solution.py:11
  850.7 63.6 %copy-start.1 = (bf16[320,1024]{1,0:T(8,128)(2,1)S(1)}, bf16[320,1024]{1,0:T(8,128)(2,1)}, u32[]{:S(2)}) copy-start(bf16[320,1024]{1,0:T(8,128)(2,1)} %param.5) | copy-start | bytes 1966084
Sparse Core Ops, SparseCore 0:
  9.8 40.1 all-gather.5
  850.8 60.8 reduce-scatter.1
where the time goes:
time: 921 us
  waiting for transfers between devices  797 us (87%)
  matrix products  35.6 us (4%)
  other arithmetic  24.8 us (3%)
  local copies, waits for them, and re-layouts  20.8 us (2%)
  starting transfers between devices  16.3 us (2%)
  between operations  14.2 us (2%)
  blocking collectives  12.7 us (1%)
    ppermute x12, waiting for transfers between devices, from_behind(): lax.ppermute(array, axis, [(i, (i + by) % peers) for i in range(peers)])  705 us
    reduce_scatter x1, waiting for transfers between devices, local(): grad_keys = lax.psum_scatter(summed, 'pb', scatter_dimension=0, tiled=True)  49.1 us
    all_gather x1, waiting for transfers between devices, local(): block_keys = lax.all_gather(key_rows, 'pb', axis=0, tiled=True)  42.1 us
  transfers between devices with their start and end apart: 14, of which 14 were waited for; matrix products, arithmetic and copies ran while one was open for 2% of the time, Pallas kernels for 0%

commit v1 on v0

v1 whole, which is shorter than its diff:
```python
import functools
import heapq

import jax
import jax.numpy as jnp
from jax import lax
from jax.experimental import pallas as pl
from jax.experimental.pallas import tpu as pltpu
from jax.sharding import PartitionSpec as P

WIN = 4
LANES = 128
LOG2E = 1.4426950408889634
LN2 = 0.6931471805599453
MESH = pl.DeviceIdType.MESH
TREES = "AAAB"
CHUNKS = len(TREES)
LINKS = {"P": 0, "M": 1, "V": 2, "C": 3}


def forwards(M, s, J, tree):
    out = []
    if tree == "A":
        if s == 0:
            if J == 0:
                out.append("P")
            out.append("V")
            if M == 0:
                out.append("M")
        elif s == 1:
            out.append("V")
        elif s == 2 and M == 1:
            out.append("M")
    else:
        if s == 0 and J == 0:
            out += ["P", "V"]
            if M == 0:
                out.append("M")
        elif s == 2 and J == 0:
            out.append("P")
            if M == 1:
                out.append("M")
        elif s == 1 and J == 1:
            out += ["P", "V"]
        elif s == 3 and J == 1:
            out.append("P")
    return out


def received(link, M, s, J):
    if link == "P":
        return (M, s, 1 - J)
    if link == "M":
        return (1 - M, 1, 1 - J)
    return (M, s + 2, J)


def depth(M, s, J, tree):
    return max([1 + depth(*received(k, M, s, J), tree) for k in forwards(M, s, J, tree)], default=0)


def plan(trees, total=14.5, lat=1.5, queue=2):
    chunks = len(trees)
    ct = total / chunks
    links = ["P", "M", "V0", "V1"]
    free = {k: 0.0 for k in links}
    flying = {k: [] for k in links}
    ready = {k: [] for k in links}
    ops, heap, count = [], [], [0]

    def have(M, s, J, n):
        for k in forwards(M, s, J, trees[n]):
            name = k if k != "V" else "V%d" % M
            count[0] += 1
            rank = -(1 + depth(*received(k, M, s, J), trees[n]))
            ready[name].append((rank, n, count[0], (k, M, s, J, n)))

    def fill(t):
        for k in links:
            flying[k] = [f for f in flying[k] if f > t + 1e-9]
            while ready[k] and len(flying[k]) < queue:
                ready[k].sort()
                item = ready[k].pop(0)[3]
                free[k] = max(free[k], t) + ct
                flying[k].append(free[k])
                ops.append(("send", t) + item)
                count[0] += 1
                heapq.heappush(heap, (free[k] + lat, count[0], received(*item[:4]) + (item[4],)))

    for n in range(chunks):
        for M in (1, 0):
            have(M, 0, 0, n)
    fill(0.0)
    while heap:
        t, _, item = heapq.heappop(heap)
        ops.append(("wait", t) + item)
        have(*item)
        fill(t)
    return ops


def with_tiles(ops, chunks, lag=2.5):
    out, left, due, done = [], {}, [], set()
    for M in (1, 0):
        left[(M, 0, 0)] = 0
        due.append((lag, (M, 0, 0)))
    for op in ops:
        ready = [d for d in due if d[0] <= op[1]]
        for d in ready:
            due.remove(d)
            out.append(("tile", op[1]) + d[1])
            done.add(d[1])
        out.append(op)
        if op[0] == "wait":
            key = op[2:5]
            left[key] = left.get(key, chunks) - 1
            if left[key] == 0:
                due.append((op[1] + lag, key))
    for d in sorted(due, key=lambda d: (-d[1][0], d[0])):
        out.append(("tile", d[0]) + d[1])
    return out


def kernel(
    blocks,
    q_hbm,
    k_hbm,
    partner_ref,
    loss_ref,
    gq_ref,
    gk_ref,
    win,
    sc,
    mx,
    sm,
    wb,
    colbuf,
    rowbuf,
    lse_col,
    par_col,
    lse_out,
    lse_in,
    par_out,
    par_in,
    load_sem,
    send_sem,
    ring_sem,
    core_sem,
    lse_send,
    lse_recv,
    par_send,
    par_recv,
):
    R, D = q_hbm.shape
    T = 2 * R
    CH = R // CHUNKS
    blk = lax.axis_index("blk")
    pb = lax.axis_index("pb")
    e = lax.rem(blk, 2)
    a = lax.div(pb, 2)
    core = lax.rem(pb, 2)
    mat = (e, 1 - e)
    cls = (a, 1 - a)
    own = pl.ds(pl.multiple_of(pb * R, 16), R)
    pair = (blk, pb + 2 - 4 * a)
    mate = (blk, pb + 1 - 2 * core)
    mirror = (blk + 1 - 2 * e, pb + 2 - 4 * a)
    cross = (blk, 3 - pb)
    up = (lax.rem(blk + 2, blocks), pb)
    down = (lax.rem(blk + blocks - 2, blocks), pb)

    load_q = pltpu.make_async_copy(q_hbm, win.at[1, 0, own], load_sem.at[0])
    load_k = pltpu.make_async_copy(k_hbm, win.at[0, 0, own], load_sem.at[1])
    load_q.start()
    load_k.start()
    barrier = pltpu.get_barrier_semaphore()
    for peer in (pair, mate, mirror, cross, up, down):
        pl.semaphore_signal(barrier, inc=1, device_id=peer, device_id_type=MESH)
    pl.semaphore_wait(barrier, 6)
    load_q.wait()
    load_k.wait()

    def slot(m, s, J, n, lane):
        at = pl.multiple_of((2 * cls[J] + lane) * R + n * CH, 16)
        return win.at[m, s, pl.ds(at, CH)]

    def copy(link, M, s, J, n):
        m, j = mat[M], cls[J]
        s_to = {"P": s, "M": 1, "V": s + 2, "C": s}[link]
        peer = {"P": pair, "M": mirror, "C": mate, "V": (lax.rem(blk + 2 - 4 * m + blocks, blocks), pb)}[link]
        sem = core_sem if link == "C" else ring_sem
        return pltpu.make_async_remote_copy(
            src_ref=slot(m, s, J, n, core),
            dst_ref=slot(m, s_to, J, n, core),
            send_sem=send_sem.at[LINKS[link], m, s, j, n],
            recv_sem=sem.at[m, s_to, j, n],
            device_id=peer,
            device_id_type=MESH,
        )

    def arrival(M, s, J, n, sem, lane, peer):
        m, j = mat[M], cls[J]
        ref = slot(m, s, J, n, lane)
        return pltpu.make_async_remote_copy(
            src_ref=ref,
            dst_ref=ref,
            send_sem=send_sem.at[0, m, s, j, n],
            recv_sem=sem.at[m, s, j, n],
            device_id=peer,
            device_id_type=MESH,
        )

    sent = []

    def start(link, M, s, J, n):
        c = copy(link, M, s, J, n)
        c.start()
        sent.append(c)

    def tile(M, s, J):
        m, j = mat[M], cls[J]
        for n in range(CHUNKS):
            arrival(M, s, J, n, core_sem, 1 - core, mate).wait_recv()
        rows = win[1 - m, 0, own, :]
        cols = win[m, s, pl.ds(pl.multiple_of(j * T, 16), T), :]
        x = lax.dot_general(rows, cols, (((1,), (1,)), ((), ())), preferred_element_type=jnp.float32)
        x = x * (LOG2E * float(D) ** -0.5)
        sc[m, s, j] = x
        parts = [x[:, g * LANES : (g + 1) * LANES] for g in range(T // LANES)]
        old = mx[m]
        new = functools.reduce(jnp.maximum, parts, old)
        total = sm[m] * jnp.exp2(old - new)
        for part in parts:
            total = total + jnp.exp2(part - new)
        mx[m] = new
        sm[m] = total

    def to_row(col):
        colbuf[pl.ds(pl.multiple_of(core * R, 8), R), :] = col
        return colbuf[...].T[0:1, :]

    ops = with_tiles(plan(TREES), CHUNKS)
    lead = [op for op in ops if op[0] == "send" and op[1] == 0.0]
    for op in lead:
        start(*op[2:])
    for n in range(CHUNKS):
        for M in (1, 0):
            start("C", M, 0, 0, n)

    colbuf[...] = jnp.zeros_like(colbuf)
    mx[...] = jnp.full_like(mx, -3.0e38)
    sm[...] = jnp.zeros_like(sm)
    rowbuf[...] = jnp.zeros_like(rowbuf)
    rowbuf[:, 0:R] = jnp.broadcast_to(partner_ref[...].astype(jnp.float32), (LANES, R))
    par_col[...] = rowbuf[...].T[0:R, :]
    row = to_row(par_col[...])
    par_out[...] = row
    par_in[pb] = row
    par_copies = []
    for i, peer in enumerate((pair, mate, cross)):
        c = pltpu.make_async_remote_copy(
            src_ref=par_out,
            dst_ref=par_in.at[pb],
            send_sem=par_send.at[i],
            recv_sem=par_recv.at[pb],
            device_id=peer,
            device_id_type=MESH,
        )
        c.start()
        par_copies.append(c)

    def lse_copy(m, s, t):
        peer = (lax.rem(blk + (2 * m - 1) * s + blocks, blocks), lax.rem(pb + t, 4))
        return pltpu.make_async_remote_copy(
            src_ref=lse_out.at[m],
            dst_ref=lse_in.at[1 - m, s, pb],
            send_sem=lse_send.at[m, s, t],
            recv_sem=lse_recv.at[1 - m, s, pb],
            device_id=peer,
            device_id_type=MESH,
        )

    lse_copies = []

    def finish(M):
        m = mat[M]
        high = mx[m]
        top = jnp.max(high, axis=1, keepdims=True)
        total = jnp.sum(sm[m] * jnp.exp2(high - top), axis=1, keepdims=True)
        lse = top + jnp.log(total) * LOG2E + 1.0
        full = jnp.broadcast_to(lse, (R, LANES))
        lse_col[m] = full
        out = to_row(full)
        lse_out[m] = out
        lse_in[1 - m, 0, pb] = out
        for s in range(WIN - 1, -1, -1):
            for t in range(4):
                if s or t:
                    c = lse_copy(m, s, t)
                    c.start()
                    lse_copies.append(c)

    waiting = {0: 4 * 2, 1: 4 * 2}
    for op in ops:
        if op[0] == "send":
            if op[1] > 0.0:
                start(*op[2:])
        elif op[0] == "wait":
            M, s, J, n = op[2:]
            arrival(M, s, J, n, ring_sem, core, pair).wait_recv()
            start("C", M, s, J, n)
        else:
            M = op[2]
            tile(*op[2:])
            waiting[M] -= 1
            if waiting[M] == 0:
                finish(M)

    for c in sent:
        c.wait_send()
    for c in par_copies:
        c.wait_send()
    for t in range(1, 4):
        p = lax.rem(pb + t, 4)
        pltpu.make_async_remote_copy(
            src_ref=par_out,
            dst_ref=par_in.at[p],
            send_sem=par_send.at[0],
            recv_sem=par_recv.at[p],
            device_id=pair,
            device_id_type=MESH,
        ).wait_recv()
    for m in range(2):
        for s in range(WIN):
            for t in range(4):
                if s or t:
                    p = lax.rem(pb + t, 4)
                    pltpu.make_async_remote_copy(
                        src_ref=lse_out.at[m],
                        dst_ref=lse_in.at[m, s, p],
                        send_sem=lse_send.at[m, s, t],
                        recv_sem=lse_recv.at[m, s, p],
                        device_id=pair,
                        device_id_type=MESH,
                    ).wait_recv()
    for c in lse_copies:
        c.wait_send()

    def weights(m, s):
        picked, partner_lse = [], []
        for j in range(2):
            c = lse_in[m, s, 2 * j] + lse_in[m, s, 2 * j + 1]
            if s == 0 and m == 1:
                chosen = par_in[2 * j] + par_in[2 * j + 1]
            for g in range(T // LANES):
                lanes = slice(g * LANES, (g + 1) * LANES)
                x = sc[m, s, j, :, lanes]
                cg = c[:, lanes]
                w = jnp.exp2(x - lse_col[m]) + jnp.exp2(x - cg)
                if s == 0:
                    if m == 0:
                        at = lax.broadcasted_iota(jnp.int32, (R, LANES), 1) + (j * T + g * LANES)
                        hit = at.astype(jnp.float32) == par_col[...]
                        picked.append(jnp.where(hit, x, 0.0))
                        partner_lse.append(jnp.where(hit, cg, 0.0))
                    else:
                        at = lax.broadcasted_iota(jnp.int32, (R, LANES), 0) + pb * R
                        hit = at.astype(jnp.float32) == chosen[:, lanes]
                    w = w - jnp.where(hit, 1.0, 0.0)
                wb[m, :, j * T + g * LANES : j * T + (g + 1) * LANES] = w.astype(jnp.bfloat16)
        if picked:
            score = jnp.sum(sum(picked), axis=1, keepdims=True)
            other = jnp.sum(sum(partner_lse), axis=1, keepdims=True)
            mine = lse_col[0][:, 0:1]
            loss = LN2 * (0.5 * (mine - 1.0) + 0.5 * (other - 1.0) - score)
            rowbuf2 = jnp.broadcast_to(loss, (R, LANES))
            colbuf[0:R, :] = rowbuf2
            loss_ref[...] = colbuf[...].T[0:1, 0:R]

    for s in range(WIN):
        for m, out in ((0, gq_ref), (1, gk_ref)):
            weights(m, s)
            part = jnp.dot(wb[m], win[m, s], preferred_element_type=jnp.float32) * float(D) ** -0.5
            if s == 0:
                out[...] = part
            else:
                out[...] += part


def local(blocks, query_rows, key_rows, partner):
    R, D = query_rows.shape
    T = 2 * R
    RP = (R + LANES - 1) // LANES * LANES
    f32, bf16 = jnp.float32, jnp.bfloat16
    dma = pltpu.SemaphoreType.DMA
    any_spec = pl.BlockSpec(memory_space=pl.ANY)
    vmem = pl.BlockSpec(memory_space=pltpu.VMEM)
    loss, grad_queries, grad_keys = pl.pallas_call(
        functools.partial(kernel, blocks),
        out_shape=(
            jax.ShapeDtypeStruct((1, R), f32),
            jax.ShapeDtypeStruct((R, D), f32),
            jax.ShapeDtypeStruct((R, D), f32),
        ),
        in_specs=[any_spec, any_spec, vmem],
        out_specs=[vmem, vmem, vmem],
        scratch_shapes=[
            pltpu.VMEM((2, WIN, 4 * R, D), bf16),
            pltpu.VMEM((2, WIN, 2, R, T), f32),
            pltpu.VMEM((2, R, LANES), f32),
            pltpu.VMEM((2, R, LANES), f32),
            pltpu.VMEM((2, R, 4 * R), bf16),
            pltpu.VMEM((T, LANES), f32),
            pltpu.VMEM((LANES, RP), f32),
            pltpu.VMEM((2, R, LANES), f32),
            pltpu.VMEM((R, LANES), f32),
            pltpu.VMEM((2, 1, T), f32),
            pltpu.VMEM((2, WIN, 4, 1, T), f32),
            pltpu.VMEM((1, T), f32),
            pltpu.VMEM((4, 1, T), f32),
            dma((2,)),
            dma((4, 2, WIN, 2, CHUNKS)),
            dma((2, WIN, 2, CHUNKS)),
            dma((2, WIN, 2, CHUNKS)),
            dma((2, WIN, 4)),
            dma((2, WIN, 4)),
            dma((3,)),
            dma((4,)),
        ],
        compiler_params=pltpu.CompilerParams(
            collective_id=0, has_side_effects=True, vmem_limit_bytes=58 * 1024 * 1024
        ),
        name="window_loss",
    )(query_rows, key_rows, partner)
    return loss.reshape(R), grad_queries, grad_keys


def solution(mesh):
    return jax.shard_map(
        functools.partial(local, mesh.shape["blk"]),
        mesh=mesh,
        in_specs=(P(("blk", "pb"), None), P(("blk", "pb"), None), P("blk", "pb")),
        out_specs=(P(("blk", "pb")), P(("blk", "pb"), None), P(("blk", "pb"), None)),
        check_vma=False,
    )
```

time: 921 us -> 98 us (0.11)
  waiting for transfers between devices: 797 us -> 0 us
  Pallas kernels: 0 us -> 92.3 us
  matrix products: 35.6 us -> 0 us
  other arithmetic: 24.8 us -> 1.26 us
  local copies, waits for them, and re-layouts: 20.8 us -> 3.69 us
  starting transfers between devices: 16.3 us -> 0 us
  between operations: 14.2 us -> 0.64 us
  blocking collectives: 12.7 us -> 0 us
    ppermute x12 -> x0, waiting for transfers between devices: 705 us -> none  [from_behind(): lax.ppermute(array, axis, [(i, (i + by) % peers) for i in range(peers)])]
    pallas_call x0 -> x1, Pallas kernels: none -> 92.3 us  [local(): pl.pallas_call(functools.partial(kernel, blocks), out_shape=(jax.ShapeDty...]
    reduce_scatter x1 -> x0, waiting for transfers between devices: 49.1 us -> none  [local(): grad_keys = lax.psum_scatter(summed, 'pb', scatter_dimension=0, tiled=True)]
    all_gather x1 -> x0, waiting for transfers between devices: 42.1 us -> none  [local(): block_keys = lax.all_gather(key_rows, 'pb', axis=0, tiled=True)]
    dot_general x3 -> x0, matrix products: 35.6 us -> none  [the longest x1 16.3 us: local(): jnp.einsum('sqk,qd->skd', weights, query_rows, preferred_element_type=jnp...]
    ppermute x12 -> x0, starting transfers between devices: 16.2 us -> none  [from_behind(): lax.ppermute(array, axis, [(i, (i + by) % peers) for i in range(peers)])]
    squeeze x2 -> x0, local copies, waits for them, and re-layouts: 13.9 us -> none  [the longest x1 12.4 us: local(): summed = summed + from_behind(partials[step], 'blk', -step)]
    add x8 -> x0, other arithmetic: 12.8 us -> none  [the longest x1 12.6 us: local(): summed = summed + from_behind(partials[step], 'blk', -step)]
  transfers between devices with their start and end apart: 14 -> 0, of which waited for: 14 -> 0; matrix products, arithmetic and copies ran while one was open for 2% -> 0% of each run, Pallas kernels for 0% -> 0%
where the time goes in v1:
time: 98 us; the launch traced here: 97.8 us
  Pallas kernels  92.3 us (94%)
  local copies, waits for them, and re-layouts  3.69 us (4%)
  other arithmetic  1.26 us (1%)
    pallas_call x1, Pallas kernels, local(): pl.pallas_call(functools.partial(kernel, blocks), out_shape=(jax.ShapeDty...  92.3 us
    unnamed x4, local copies, waits for them, and re-layouts  3.69 us

profile of v1, /device:TPU:1, one launch (start us, length us, event | category | flops | bytes accessed | tf_op | source)
XLA Modules:
  0.0 97.8 jit_solution(15674233644674328258)
XLA Ops:
  0.6 92.3 %window_loss.1 = (f32[1,320]{1,0:T(1,128)}, f32[320,1024]{1,0:T(8,128)}, f32[320,1024]{1,0:T(8,128)}) custom-call(bf16[320,1024]{1,0:T(8,128)(2,1)} %q_hbm.1, bf16[320,1024]{1,0:T(8,128)(2,1)} %k_hbm.1, s32[1,320]{1,0:T(1,128)} %partner_ref.1), custom_call_target="tpu_custom_call" | custom-call | tf_op jit(solution)/shard_map/window_loss/pallas_call | solution.py:398
  92.9 1.3 %reduce = f32[320]{0:T(512)} reduce(f32[1,320]{1,0:T(1,128)} %get-tuple-element.6, f32[]{:T(128)} %constant.3), dimensions={0}, to_apply=%get-tuple-element.6.reduce_sub_computation | reduce | bytes 2564 | tf_op jit(solution)/shard_map/window_loss/pallas_call | solution.py:398
  94.2 0.0 copy-start
  94.2 2.6 %copy.8 = f32[320,1024]{1,0:T(8,128)} copy(f32[320,1024]{1,0:T(8,128)} %get-tuple-element.13) | data formatting | bytes 2621440
  96.8 0.0 copy-done
  96.8 1.1 %copy.9 = f32[320,1024]{1,0:T(8,128)} copy(f32[320,1024]{1,0:T(8,128)S(1)} %copy-done) | data formatting | bytes 2621440
Async XLA Ops:
  94.2 2.6 %copy-start = (f32[320,1024]{1,0:T(8,128)S(1)}, f32[320,1024]{1,0:T(8,128)}, u32[]{:S(2)}) copy-start(f32[320,1024]{1,0:T(8,128)} %get-tuple-element.14) | copy-start | bytes 3932164

commit v2 on v1

--- a/solution.py
+++ b/solution.py
@@ -13,37 +13,40 @@
 LOG2E = 1.4426950408889634
 LN2 = 0.6931471805599453
 MESH = pl.DeviceIdType.MESH
-TREES = "AAAB"
+TREES = "BAD"
+SIZES = (48, 160, 112)
 CHUNKS = len(TREES)
 LINKS = {"P": 0, "M": 1, "V": 2, "C": 3}
+PRIORITY = {
+    "P": ((3.2, 3.7, 0.4, 1.3), (3.6, 0.3, 1.4, 4.2)),
+    "M": ((2.3, 0.0, 0.0, 0.0), (0.0, 0.0, 2.2, 0.0)),
+    "V0": ((2.0, 0.7, 0.0, 0.0), (0.0, 0.0, 0.0, 0.0)),
+    "V1": ((0.0, 0.0, 0.0, 0.0), (2.6, 3.1, 0.0, 0.0)),
+}
+LATENCY = {"P": 1.7, "M": 2.0, "V": 2.6}
 
 
 def forwards(M, s, J, tree):
     out = []
-    if tree == "A":
-        if s == 0:
-            if J == 0:
-                out.append("P")
+    if s == 0:
+        if J == 0:
+            out.append("P")
+        if J == 0 or tree != "B":
             out.append("V")
             if M == 0:
                 out.append("M")
-        elif s == 1:
+    elif s == 1:
+        if tree == "A":
             out.append("V")
-        elif s == 2 and M == 1:
+        elif J == 1:
+            out += ["P", "V"] if tree == "B" else ["V"]
+    elif s == 2:
+        if tree == "B" and J == 0:
+            out.append("P")
+        if M == 1 and (J == 0 or tree != "B"):
             out.append("M")
-    else:
-        if s == 0 and J == 0:
-            out += ["P", "V"]
-            if M == 0:
-                out.append("M")
-        elif s == 2 and J == 0:
-            out.append("P")
-            if M == 1:
-                out.append("M")
-        elif s == 1 and J == 1:
-            out += ["P", "V"]
-        elif s == 3 and J == 1:
-            out.append("P")
+    elif J == 1 and tree != "A":
+        out.append("P")
     return out
 
 
@@ -55,13 +58,9 @@
     return (M, s + 2, J)
 
 
-def depth(M, s, J, tree):
-    return max([1 + depth(*received(k, M, s, J), tree) for k in forwards(M, s, J, tree)], default=0)
-
-
-def plan(trees, total=14.5, lat=1.5, queue=2):
+def plan(trees, queue=2):
     chunks = len(trees)
-    ct = total / chunks
+    ct = [2 * (rows * 2048e-5 + 0.15) for rows in SIZES]
     links = ["P", "M", "V0", "V1"]
     free = {k: 0.0 for k in links}
     flying = {k: [] for k in links}
@@ -71,9 +70,7 @@
     def have(M, s, J, n):
         for k in forwards(M, s, J, trees[n]):
             name = k if k != "V" else "V%d" % M
-            count[0] += 1
-            rank = -(1 + depth(*received(k, M, s, J), trees[n]))
-            ready[name].append((rank, n, count[0], (k, M, s, J, n)))
+            ready[name].append((n - PRIORITY[name][M][s], n, J, (k, M, s, J, n)))
 
     def fill(t):
         for k in links:
@@ -81,11 +78,11 @@
             while ready[k] and len(flying[k]) < queue:
                 ready[k].sort()
                 item = ready[k].pop(0)[3]
-                free[k] = max(free[k], t) + ct
+                free[k] = max(free[k], t) + ct[item[4]]
                 flying[k].append(free[k])
                 ops.append(("send", t) + item)
                 count[0] += 1
-                heapq.heappush(heap, (free[k] + lat, count[0], received(*item[:4]) + (item[4],)))
+                heapq.heappush(heap, (free[k] + LATENCY[item[0]], count[0], received(*item[:4]) + (item[4],)))
 
     for n in range(chunks):
         for M in (1, 0):
@@ -99,7 +96,7 @@
     return ops
 
 
-def with_tiles(ops, chunks, lag=2.5):
+def with_tiles(ops, chunks, lag=1.6):
     out, left, due, done = [], {}, [], set()
     for M in (1, 0):
         left[(M, 0, 0)] = 0
@@ -125,10 +122,9 @@
     blocks,
     q_hbm,
     k_hbm,
-    partner_ref,
+    partner_hbm,
     loss_ref,
-    gq_ref,
-    gk_ref,
+    grad_ref,
     win,
     sc,
     mx,
@@ -142,6 +138,7 @@
     lse_in,
     par_out,
     par_in,
+    partner_ref,
     load_sem,
     send_sem,
     ring_sem,
@@ -153,7 +150,8 @@
 ):
     R, D = q_hbm.shape
     T = 2 * R
-    CH = R // CHUNKS
+    starts = [sum(SIZES[:n]) for n in range(CHUNKS)]
+    assert sum(SIZES) == R
     blk = lax.axis_index("blk")
     pb = lax.axis_index("pb")
     e = lax.rem(blk, 2)
@@ -171,18 +169,21 @@
 
     load_q = pltpu.make_async_copy(q_hbm, win.at[1, 0, own], load_sem.at[0])
     load_k = pltpu.make_async_copy(k_hbm, win.at[0, 0, own], load_sem.at[1])
+    load_p = pltpu.make_async_copy(partner_hbm, partner_ref, load_sem.at[2])
     load_q.start()
     load_k.start()
+    load_p.start()
     barrier = pltpu.get_barrier_semaphore()
     for peer in (pair, mate, mirror, cross, up, down):
         pl.semaphore_signal(barrier, inc=1, device_id=peer, device_id_type=MESH)
     pl.semaphore_wait(barrier, 6)
     load_q.wait()
     load_k.wait()
+    load_p.wait()
 
     def slot(m, s, J, n, lane):
-        at = pl.multiple_of((2 * cls[J] + lane) * R + n * CH, 16)
-        return win.at[m, s, pl.ds(at, CH)]
+        at = pl.multiple_of((2 * cls[J] + lane) * R + starts[n], 16)
+        return win.at[m, s, pl.ds(at, SIZES[n])]
 
     def copy(link, M, s, J, n):
         m, j = mat[M], cls[J]
@@ -330,80 +331,96 @@
             device_id=pair,
             device_id_type=MESH,
         ).wait_recv()
-    for m in range(2):
-        for s in range(WIN):
-            for t in range(4):
-                if s or t:
-                    p = lax.rem(pb + t, 4)
-                    pltpu.make_async_remote_copy(
-                        src_ref=lse_out.at[m],
-                        dst_ref=lse_in.at[m, s, p],
-                        send_sem=lse_send.at[m, s, t],
-                        recv_sem=lse_recv.at[m, s, p],
-                        device_id=pair,
-                        device_id_type=MESH,
-                    ).wait_recv()
-    for c in lse_copies:
-        c.wait_send()
-
-    def weights(m, s):
-        picked, partner_lse = [], []
+    def lse_wait(M, s):
+        m = mat[M]
+        for t in range(4):
+            if s or t:
+                p = lax.rem(pb + t, 4)
+                pltpu.make_async_remote_copy(
+                    src_ref=lse_out.at[m],
+                    dst_ref=lse_in.at[m, s, p],
+                    send_sem=lse_send.at[m, s, t],
+                    recv_sem=lse_recv.at[m, s, p],
+                    device_id=pair,
+                    device_id_type=MESH,
+                ).wait_recv()
+
+    def gradient(M, s, first):
+        m = mat[M]
+        keys = mat[M] == 0
         for j in range(2):
             c = lse_in[m, s, 2 * j] + lse_in[m, s, 2 * j + 1]
-            if s == 0 and m == 1:
+            if s == 0:
                 chosen = par_in[2 * j] + par_in[2 * j + 1]
             for g in range(T // LANES):
                 lanes = slice(g * LANES, (g + 1) * LANES)
                 x = sc[m, s, j, :, lanes]
-                cg = c[:, lanes]
-                w = jnp.exp2(x - lse_col[m]) + jnp.exp2(x - cg)
+                w = jnp.exp2(x - lse_col[m]) + jnp.exp2(x - c[:, lanes])
                 if s == 0:
-                    if m == 0:
-                        at = lax.broadcasted_iota(jnp.int32, (R, LANES), 1) + (j * T + g * LANES)
-                        hit = at.astype(jnp.float32) == par_col[...]
-                        picked.append(jnp.where(hit, x, 0.0))
-                        partner_lse.append(jnp.where(hit, cg, 0.0))
-                    else:
-                        at = lax.broadcasted_iota(jnp.int32, (R, LANES), 0) + pb * R
-                        hit = at.astype(jnp.float32) == chosen[:, lanes]
+                    col = lax.broadcasted_iota(jnp.int32, (R, LANES), 1) + (j * T + g * LANES)
+                    row = lax.broadcasted_iota(jnp.int32, (R, LANES), 0) + pb * R
+                    at = jnp.where(keys, col, row).astype(jnp.float32)
+                    hit = at == jnp.where(keys, par_col[...], jnp.broadcast_to(chosen[:, lanes], (R, LANES)))
                     w = w - jnp.where(hit, 1.0, 0.0)
                 wb[m, :, j * T + g * LANES : j * T + (g + 1) * LANES] = w.astype(jnp.bfloat16)
-        if picked:
-            score = jnp.sum(sum(picked), axis=1, keepdims=True)
-            other = jnp.sum(sum(partner_lse), axis=1, keepdims=True)
-            mine = lse_col[0][:, 0:1]
-            loss = LN2 * (0.5 * (mine - 1.0) + 0.5 * (other - 1.0) - score)
-            rowbuf2 = jnp.broadcast_to(loss, (R, LANES))
-            colbuf[0:R, :] = rowbuf2
-            loss_ref[...] = colbuf[...].T[0:1, 0:R]
-
-    for s in range(WIN):
-        for m, out in ((0, gq_ref), (1, gk_ref)):
-            weights(m, s)
-            part = jnp.dot(wb[m], win[m, s], preferred_element_type=jnp.float32) * float(D) ** -0.5
-            if s == 0:
-                out[...] = part
-            else:
-                out[...] += part
+        part = jnp.dot(wb[m], win[m, s], preferred_element_type=jnp.float32)
+        if first:
+            grad_ref[m] = part
+        else:
+            grad_ref[m] += part
+
+    for M, s in ((1, 1), (1, 3), (0, 0), (0, 2)):
+        lse_wait(M, s)
+    gradient(1, 1, True)
+    gradient(0, 0, True)
+    gradient(1, 3, False)
+    gradient(0, 2, False)
+    for M, s in ((1, 0), (1, 2), (0, 1), (0, 3)):
+        lse_wait(M, s)
+    for c in lse_copies:
+        c.wait_send()
+    gradient(1, 2, False)
+    gradient(0, 1, False)
+    gradient(1, 0, False)
+    gradient(0, 3, False)
+
+    picked = jnp.zeros((R, LANES), jnp.float32)
+    partner_lse = picked
+    for j in range(2):
+        c = lse_in[0, 0, 2 * j] + lse_in[0, 0, 2 * j + 1]
+        for g in range(T // LANES):
+            lanes = slice(g * LANES, (g + 1) * LANES)
+            col = lax.broadcasted_iota(jnp.int32, (R, LANES), 1) + (j * T + g * LANES)
+            hit = col.astype(jnp.float32) == par_col[...]
+            picked += jnp.where(hit, sc[0, 0, j, :, lanes], 0.0)
+            partner_lse += jnp.where(hit, jnp.broadcast_to(c[:, lanes], (R, LANES)), 0.0)
+    score = jnp.sum(picked, axis=1, keepdims=True)
+    other = jnp.sum(partner_lse, axis=1, keepdims=True)
+    mine = lse_col[0][:, 0:1]
+    loss = LN2 * (0.5 * (mine - 1.0) + 0.5 * (other - 1.0) - score)
+    colbuf[0:R, :] = jnp.broadcast_to(loss, (R, LANES))
+    loss_ref[...] = colbuf[...].T[0:1, 0:R]
 
 
 def local(blocks, query_rows, key_rows, partner):
+    query_rows = pltpu.with_memory_space_constraint(query_rows, pltpu.HBM)
+    key_rows = pltpu.with_memory_space_constraint(key_rows, pltpu.HBM)
+    partner = pltpu.with_memory_space_constraint(partner, pltpu.HBM)
     R, D = query_rows.shape
     T = 2 * R
     RP = (R + LANES - 1) // LANES * LANES
     f32, bf16 = jnp.float32, jnp.bfloat16
     dma = pltpu.SemaphoreType.DMA
-    any_spec = pl.BlockSpec(memory_space=pl.ANY)
+    hbm = pl.BlockSpec(memory_space=pltpu.HBM)
     vmem = pl.BlockSpec(memory_space=pltpu.VMEM)
-    loss, grad_queries, grad_keys = pl.pallas_call(
+    loss, grads = pl.pallas_call(
         functools.partial(kernel, blocks),
         out_shape=(
             jax.ShapeDtypeStruct((1, R), f32),
-            jax.ShapeDtypeStruct((R, D), f32),
-            jax.ShapeDtypeStruct((R, D), f32),
+            jax.ShapeDtypeStruct((2, R, D), f32),
         ),
-        in_specs=[any_spec, any_spec, vmem],
-        out_specs=[vmem, vmem, vmem],
+        in_specs=[hbm, hbm, hbm],
+        out_specs=[vmem, vmem],
         scratch_shapes=[
             pltpu.VMEM((2, WIN, 4 * R, D), bf16),
             pltpu.VMEM((2, WIN, 2, R, T), f32),
@@ -418,7 +435,8 @@
             pltpu.VMEM((2, WIN, 4, 1, T), f32),
             pltpu.VMEM((1, T), f32),
             pltpu.VMEM((4, 1, T), f32),
-            dma((2,)),
+            pltpu.VMEM((1, R), jnp.int32),
+            dma((3,)),
             dma((4, 2, WIN, 2, CHUNKS)),
             dma((2, WIN, 2, CHUNKS)),
             dma((2, WIN, 2, CHUNKS)),
@@ -428,11 +446,12 @@
             dma((4,)),
         ],
         compiler_params=pltpu.CompilerParams(
-            collective_id=0, has_side_effects=True, vmem_limit_bytes=58 * 1024 * 1024
+            collective_id=0, has_side_effects=True, vmem_limit_bytes=46 * 1024 * 1024
         ),
         name="window_loss",
     )(query_rows, key_rows, partner)
-    return loss.reshape(R), grad_queries, grad_keys
+    factor = float(D) ** -0.5
+    return loss.reshape(R), grads[0] * factor, grads[1] * factor
 
 
 def solution(mesh):

time: 98 us -> 88.1 us (0.90)
  Pallas kernels: 92.3 us -> 85 us
  local copies, waits for them, and re-layouts: 3.69 us -> 0 us
  other arithmetic: 1.26 us -> 2.37 us
    pallas_call x1, Pallas kernels: 92.3 us -> 85 us  [local(): pl.pallas_call(functools.partial(kernel, blocks), out_shape=(jax.ShapeDty...]
    unnamed x4 -> x0, local copies, waits for them, and re-layouts: 3.69 us -> none
    mul x0 -> x1, other arithmetic: none -> 1.78 us  [local(): return (loss.reshape(R), grads[0] * factor, grads[1] * factor)]
where the time goes in v2:
time: 88.1 us; the launch traced here: 88 us
  Pallas kernels  85 us (96%)
  other arithmetic  2.37 us (3%)
    pallas_call x1, Pallas kernels, local(): pl.pallas_call(functools.partial(kernel, blocks), out_shape=(jax.ShapeDty...  85 us
    mul x1, other arithmetic, local(): return (loss.reshape(R), grads[0] * factor, grads[1] * factor)  1.78 us

profile of v2, /device:TPU:1, one launch (start us, length us, event | category | flops | bytes accessed | tf_op | source)
XLA Modules:
  0.0 88.0 jit_solution(6616337181599996698)
XLA Ops:
  0.6 85.0 %window_loss.1 = (f32[1,320]{1,0:T(1,128)S(1)}, f32[2,320,1024]{2,1,0:T(8,128)S(1)}) custom-call(bf16[320,1024]{1,0:T(8,128)(2,1)} %q_hbm.1, bf16[320,1024]{1,0:T(8,128)(2,1)} %k_hbm.1, s32[1,320]{1,0:T(1,128)} %partner_hbm.1), custom_call_target="tpu_custom_call" | custom-call | tf_op jit(solution)/shard_map/window_loss/pallas_call | solution.py:416
  85.6 1.8 %multiply_bitcast_fusion = (f32[320,1024]{1,0:T(8,128)}, f32[320,1024]{1,0:T(8,128)}) fusion(f32[2,320,1024]{2,1,0:T(8,128)S(1)} %get-tuple-element.6), kind=kLoop, calls=%fused_computation | loop fusion | flops 655360 | bytes 5242880 | tf_op jit(solution)/shard_map/mul | solution.py:454
  87.4 0.6 reduce

commit v3 on v2

--- a/solution.py
+++ b/solution.py
@@ -13,41 +13,40 @@
 LOG2E = 1.4426950408889634
 LN2 = 0.6931471805599453
 MESH = pl.DeviceIdType.MESH
-TREES = "BAD"
-SIZES = (48, 160, 112)
+TREES = "ADC"
+SIZES = (48, 176, 96)
 CHUNKS = len(TREES)
 LINKS = {"P": 0, "M": 1, "V": 2, "C": 3}
 PRIORITY = {
-    "P": ((3.2, 3.7, 0.4, 1.3), (3.6, 0.3, 1.4, 4.2)),
-    "M": ((2.3, 0.0, 0.0, 0.0), (0.0, 0.0, 2.2, 0.0)),
-    "V0": ((2.0, 0.7, 0.0, 0.0), (0.0, 0.0, 0.0, 0.0)),
-    "V1": ((0.0, 0.0, 0.0, 0.0), (2.6, 3.1, 0.0, 0.0)),
+    "P": ((0.6, 3.4, 4.1, 3.0), (0.2, 1.1, 3.9, 2.4)),
+    "M": ((1.3, 0.0, 0.0, 0.0), (0.0, 0.0, 4.9, 0.0)),
+    "V0": ((0.9, 1.7, 0.0, 0.0), (0.0, 0.0, 0.0, 0.0)),
+    "V1": ((0.0, 0.0, 0.0, 0.0), (0.3, 1.6, 0.0, 0.0)),
 }
+LAGS = (4.0, 4.0)
 LATENCY = {"P": 1.7, "M": 2.0, "V": 2.6}
 
 
 def forwards(M, s, J, tree):
-    out = []
+    own = M == 0
     if s == 0:
         if J == 0:
-            out.append("P")
-        if J == 0 or tree != "B":
-            out.append("V")
-            if M == 0:
-                out.append("M")
-    elif s == 1:
-        if tree == "A":
-            out.append("V")
-        elif J == 1:
-            out += ["P", "V"] if tree == "B" else ["V"]
-    elif s == 2:
-        if tree == "B" and J == 0:
-            out.append("P")
-        if M == 1 and (J == 0 or tree != "B"):
+            return ["P", "V", "M"] if own else ["P", "V"]
+        if tree == "B":
+            return []
+        return ["V", "M"] if own and tree != "C" else ["V"]
+    if s == 1:
+        if tree == "A" or tree == "D":
+            return ["V"] if J == 1 or tree == "A" else []
+        if J == 1:
+            return ["P", "V"]
+        return ["V"] if tree == "C" else []
+    if s == 2:
+        out = ["P"] if tree == "B" and J == 0 else []
+        if not own and (J == 0 or tree in "AD"):
             out.append("M")
-    elif J == 1 and tree != "A":
-        out.append("P")
-    return out
+        return out
+    return ["P"] if J == 1 and tree in "BD" else []
 
 
 def received(link, M, s, J):
@@ -96,23 +95,22 @@
     return ops
 
 
-def with_tiles(ops, chunks, lag=1.6):
-    out, left, due, done = [], {}, [], set()
+def with_tiles(ops, chunks, lags):
+    out, left, due = [], {}, []
     for M in (1, 0):
         left[(M, 0, 0)] = 0
-        due.append((lag, (M, 0, 0)))
+        due.append((lags[M], (M, 0, 0)))
     for op in ops:
         ready = [d for d in due if d[0] <= op[1]]
         for d in ready:
             due.remove(d)
             out.append(("tile", op[1]) + d[1])
-            done.add(d[1])
         out.append(op)
         if op[0] == "wait":
             key = op[2:5]
             left[key] = left.get(key, chunks) - 1
             if left[key] == 0:
-                due.append((op[1] + lag, key))
+                due.append((op[1] + lags[op[2]], key))
     for d in sorted(due, key=lambda d: (-d[1][0], d[0])):
         out.append(("tile", d[0]) + d[1])
     return out
@@ -213,10 +211,14 @@
 
     sent = []
 
-    def start(link, M, s, J, n):
+    def start(t, link, M, s, J, n):
         c = copy(link, M, s, J, n)
         c.start()
-        sent.append(c)
+        sent.append((t, c))
+
+    def settle(t):
+        while sent and sent[0][0] + 14.0 < t:
+            sent.pop(0)[1].wait_send()
 
     def tile(M, s, J):
         m, j = mat[M], cls[J]
@@ -240,13 +242,13 @@
         colbuf[pl.ds(pl.multiple_of(core * R, 8), R), :] = col
         return colbuf[...].T[0:1, :]
 
-    ops = with_tiles(plan(TREES), CHUNKS)
+    ops = with_tiles(plan(TREES), CHUNKS, LAGS)
     lead = [op for op in ops if op[0] == "send" and op[1] == 0.0]
     for op in lead:
-        start(*op[2:])
+        start(*op[1:])
     for n in range(CHUNKS):
         for M in (1, 0):
-            start("C", M, 0, 0, n)
+            start(0.0, "C", M, 0, 0, n)
 
     colbuf[...] = jnp.zeros_like(colbuf)
     mx[...] = jnp.full_like(mx, -3.0e38)
@@ -305,11 +307,12 @@
     for op in ops:
         if op[0] == "send":
             if op[1] > 0.0:
-                start(*op[2:])
+                start(*op[1:])
         elif op[0] == "wait":
             M, s, J, n = op[2:]
             arrival(M, s, J, n, ring_sem, core, pair).wait_recv()
-            start("C", M, s, J, n)
+            start(op[1], "C", M, s, J, n)
+            settle(op[1])
         else:
             M = op[2]
             tile(*op[2:])
@@ -317,10 +320,6 @@
             if waiting[M] == 0:
                 finish(M)
 
-    for c in sent:
-        c.wait_send()
-    for c in par_copies:
-        c.wait_send()
     for t in range(1, 4):
         p = lax.rem(pb + t, 4)
         pltpu.make_async_remote_copy(
@@ -345,7 +344,7 @@
                     device_id_type=MESH,
                 ).wait_recv()
 
-    def gradient(M, s, first):
+    def weights(k, M, s):
         m = mat[M]
         keys = mat[M] == 0
         for j in range(2):
@@ -362,44 +361,49 @@
                     at = jnp.where(keys, col, row).astype(jnp.float32)
                     hit = at == jnp.where(keys, par_col[...], jnp.broadcast_to(chosen[:, lanes], (R, LANES)))
                     w = w - jnp.where(hit, 1.0, 0.0)
-                wb[m, :, j * T + g * LANES : j * T + (g + 1) * LANES] = w.astype(jnp.bfloat16)
-        part = jnp.dot(wb[m], win[m, s], preferred_element_type=jnp.float32)
+                wb[k % 2, :, j * T + g * LANES : j * T + (g + 1) * LANES] = w.astype(jnp.bfloat16)
+
+    def product(k, M, s, first):
+        m = mat[M]
+        part = jnp.dot(wb[k % 2], win[m, s], preferred_element_type=jnp.float32)
         if first:
             grad_ref[m] = part
         else:
             grad_ref[m] += part
 
-    for M, s in ((1, 1), (1, 3), (0, 0), (0, 2)):
-        lse_wait(M, s)
-    gradient(1, 1, True)
-    gradient(0, 0, True)
-    gradient(1, 3, False)
-    gradient(0, 2, False)
-    for M, s in ((1, 0), (1, 2), (0, 1), (0, 3)):
-        lse_wait(M, s)
-    for c in lse_copies:
+    def losses():
+        picked = jnp.zeros((R, LANES), jnp.float32)
+        partner_lse = picked
+        for j in range(2):
+            c = lse_in[0, 0, 2 * j] + lse_in[0, 0, 2 * j + 1]
+            for g in range(T // LANES):
+                lanes = slice(g * LANES, (g + 1) * LANES)
+                col = lax.broadcasted_iota(jnp.int32, (R, LANES), 1) + (j * T + g * LANES)
+                hit = col.astype(jnp.float32) == par_col[...]
+                picked += jnp.where(hit, sc[0, 0, j, :, lanes], 0.0)
+                partner_lse += jnp.where(hit, jnp.broadcast_to(c[:, lanes], (R, LANES)), 0.0)
+        score = jnp.sum(picked, axis=1, keepdims=True)
+        other = jnp.sum(partner_lse, axis=1, keepdims=True)
+        mine = lse_col[0][:, 0:1]
+        loss = LN2 * (0.5 * (mine - 1.0) + 0.5 * (other - 1.0) - score)
+        colbuf[0:R, :] = jnp.broadcast_to(loss, (R, LANES))
+        loss_ref[...] = colbuf[...].T[0:1, 0:R]
+
+    order = ((0, 0), (0, 2), (1, 1), (1, 3), (1, 0), (1, 2), (0, 1), (0, 3))
+    lse_wait(*order[0])
+    weights(0, *order[0])
+    seen = set()
+    for k, (M, s) in enumerate(order):
+        if k + 1 < len(order):
+            lse_wait(*order[k + 1])
+        product(k, M, s, M not in seen)
+        seen.add(M)
+        if k + 1 < len(order):
+            weights(k + 1, *order[k + 1])
+        if k == 4:
+            losses()
+    for c in [c for _, c in sent] + par_copies + lse_copies:
         c.wait_send()
-    gradient(1, 2, False)
-    gradient(0, 1, False)
-    gradient(1, 0, False)
-    gradient(0, 3, False)
-
-    picked = jnp.zeros((R, LANES), jnp.float32)
-    partner_lse = picked
-    for j in range(2):
-        c = lse_in[0, 0, 2 * j] + lse_in[0, 0, 2 * j + 1]
-        for g in range(T // LANES):
-            lanes = slice(g * LANES, (g + 1) * LANES)
-            col = lax.broadcasted_iota(jnp.int32, (R, LANES), 1) + (j * T + g * LANES)
-            hit = col.astype(jnp.float32) == par_col[...]
-            picked += jnp.where(hit, sc[0, 0, j, :, lanes], 0.0)
-            partner_lse += jnp.where(hit, jnp.broadcast_to(c[:, lanes], (R, LANES)), 0.0)
-    score = jnp.sum(picked, axis=1, keepdims=True)
-    other = jnp.sum(partner_lse, axis=1, keepdims=True)
-    mine = lse_col[0][:, 0:1]
-    loss = LN2 * (0.5 * (mine - 1.0) + 0.5 * (other - 1.0) - score)
-    colbuf[0:R, :] = jnp.broadcast_to(loss, (R, LANES))
-    loss_ref[...] = colbuf[...].T[0:1, 0:R]
 
 
 def local(blocks, query_rows, key_rows, partner):

time: 88.1 us -> 84.5 us (0.959)
  Pallas kernels: 85 us -> 81.4 us
    pallas_call x1, Pallas kernels: 85 us -> 81.4 us  [local(): pl.pallas_call(functools.partial(kernel, blocks), out_shape=(jax.ShapeDty...]
where the time goes in v3:
time: 84.5 us; the launch traced here: 84.4 us
  Pallas kernels  81.4 us (96%)
  other arithmetic  2.37 us (3%)
    pallas_call x1, Pallas kernels, local(): pl.pallas_call(functools.partial(kernel, blocks), out_shape=(jax.ShapeDty...  81.4 us
    mul x1, other arithmetic, local(): return (loss.reshape(R), grads[0] * factor, grads[1] * factor)  1.78 us

profile of v3, /device:TPU:1, one launch (start us, length us, event | category | flops | bytes accessed | tf_op | source)
XLA Modules:
  0.0 84.4 jit_solution(2675032384075320725)
XLA Ops:
  0.6 81.4 %window_loss.1 = (f32[1,320]{1,0:T(1,128)S(1)}, f32[2,320,1024]{2,1,0:T(8,128)S(1)}) custom-call(bf16[320,1024]{1,0:T(8,128)(2,1)} %q_hbm.1, bf16[320,1024]{1,0:T(8,128)(2,1)} %k_hbm.1, s32[1,320]{1,0:T(1,128)} %partner_hbm.1), custom_call_target="tpu_custom_call" | custom-call | tf_op jit(solution)/shard_map/window_loss/pallas_call | solution.py:420
  82.1 1.8 %multiply_bitcast_fusion = (f32[320,1024]{1,0:T(8,128)}, f32[320,1024]{1,0:T(8,128)}) fusion(f32[2,320,1024]{2,1,0:T(8,128)S(1)} %get-tuple-element.6), kind=kLoop, calls=%fused_computation | loop fusion | flops 655360 | bytes 5242880 | tf_op jit(solution)/shard_map/mul | solution.py:458
  83.8 0.6 reduce
